TPU v7x, 32 devices: a whole 2x2x4 slice. The times are simulated.
32 devices in a mesh: prow: 4 (over y, x), pcol: 8 (over z, core).
Axes of the slice: x: 2, y: 2, z: 4, core: 2. Of those that a mesh axis runs over, the one named last changes fastest.
Arguments:
- schur: float32 [4, 4, 128, 2, 8, 128], P(None, 'prow', None, None, 'pcol'), may hold values from -0.125 to 0.125
- panel_inverse: float32 [2, 8, 128, 2, 4, 128], P(None, 'pcol', None, None, 'prow'), may hold values from -0.1875 to 0.1875
- coupling: float32 [4, 4, 128, 256], P(None, 'prow'), may hold values from -6 to 6
- zslab: float32 [4, 4, 128, 2, 8, 128], P(None, 'prow', None, None, 'pcol')
- targets: int32 [128], replicated, may hold values from 0 to 254
- pair_flags: int32 [128], replicated, may hold values 0 or 1
Outputs:
- eigenvectors: float32 [4, 4, 128, 128], P(None, 'prow', 'pcol')
All inputs are finite; a program needn't handle non-finite values.
Results may differ from a plain program's by a relative error of at most 0.0001.
Values sent between devices are 32-bit elements; how exact they have to be, the bound alone decides.
A program may use at most 64 MiB of HBM per device.

v0:
```python
import jax
import jax.numpy as jnp
from jax import lax
from jax.sharding import PartitionSpec as P

EPSILON = 1e-06


def shards(schur, panel_inverse, coupling, zslab, targets, pair_flags):
    block_size = schur.shape[2]
    row_blocks = schur.shape[0]
    col_blocks = schur.shape[3]
    ratio_rows = panel_inverse.shape[3]
    window = coupling.shape[3]
    vector_count = targets.shape[0]
    zrow_blocks = zslab.shape[0]
    panel_rows = ratio_rows * block_size
    triangle = schur.reshape(row_blocks * block_size, col_blocks * block_size)
    inverse = panel_inverse.reshape(col_blocks, block_size, panel_rows)
    strip_rows = coupling.reshape(row_blocks * block_size, window)
    z_rows = zslab.reshape(zrow_blocks * block_size, col_blocks * block_size)
    columns = jnp.arange(window, dtype=jnp.int32)[:, None]
    selection = (columns == targets[None, :]).astype(jnp.float32) + pair_flags[None, :].astype(
        jnp.float32
    ) * (columns == targets[None, :] + 1).astype(jnp.float32)
    right_side = -jnp.dot(strip_rows, selection, precision=lax.Precision.HIGHEST)
    pieces = [None] * col_blocks
    for panel_index in reversed(range(col_blocks)):
        residual = right_side[panel_index * panel_rows : (panel_index + 1) * panel_rows]
        if panel_index < col_blocks - 1:
            later_rows = jnp.concatenate(pieces[panel_index + 1 :], axis=0)
            partial_value = jnp.dot(
                triangle[
                    panel_index * panel_rows : (panel_index + 1) * panel_rows,
                    (panel_index + 1) * block_size :,
                ],
                later_rows,
                precision=lax.Precision.HIGHEST,
            )
            residual = residual - lax.psum(partial_value, "pcol")
        applied = jnp.dot(inverse[panel_index], residual, precision=lax.Precision.HIGHEST)
        pieces[panel_index] = lax.psum(applied, "prow")
    transformed = jnp.dot(z_rows, jnp.concatenate(pieces, axis=0), precision=lax.Precision.HIGHEST)
    stacked = transformed.reshape(zrow_blocks, 1, block_size, vector_count)
    total_rows = zrow_blocks * block_size * lax.axis_size("prow")
    summed = lax.psum(stacked, "pcol")
    squares = lax.psum(jnp.sum(summed * summed, axis=(0, 1, 2)), "prow")
    share_rows = block_size // lax.axis_size("pcol")
    owned_rows = lax.dynamic_slice_in_dim(
        summed, lax.axis_index("pcol") * share_rows, share_rows, 2
    )
    divisor = jnp.sqrt(squares / total_rows + EPSILON)
    return owned_rows / divisor[None, None, None, :]


def solution(mesh):
    in_specs = (
        P(None, "prow", None, None, "pcol", None),
        P(None, "pcol", None, None, "prow", None),
        P(None, "prow", None, None),
        P(None, "prow", None, None, "pcol", None),
        P(),
        P(),
    )
    out_specs = P(None, "prow", "pcol", None)
    return jax.shard_map(shards, mesh=mesh, in_specs=in_specs, out_specs=out_specs, check_vma=False)
```

profile of v0, /device:TPU:0, one launch (start us, length us, event | category | flops | bytes accessed | tf_op | source)
XLA Modules:
  0.0 233.2 jit_solution(16619724533023797762)
XLA Ops:
  6.5 0.0 copy-start
  6.5 0.0 copy-start.5
  6.5 0.0 all-reduce.5.cloned.1.call-start
  6.5 1.8 slice_reduce_fusion
  8.4 0.0 copy-done.5
  8.4 0.0 copy-start.4
  8.4 0.6 copy-done.4
  9.1 0.0 copy-done
  9.1 0.7 fusion
  9.8 0.9 convolution_bitcast_fusion.3
  10.7 0.0 all-reduce.5.cloned.1.call-update
  10.7 0.0 all-reduce.7.cloned.1.call-start
  10.8 0.0 copy-done.2
  10.8 0.0 copy-start.1
  10.8 44.6 %all-reduce.5.cloned.1.call-done = f32[128,128]{0,1:T(8,128)} async-done(((f32[128,128]{0,1:T(8,128)}), f32[128,128]{0,1:T(8,128)}) %all-reduce.5.cloned.1.call-update) | async-done | bytes 65552 | tf_op jit(solution)/shard_map/psum | solution.py:42
  55.4 1.8 convolution_bitcast_fusion.1
  57.2 0.0 all-reduce.7.cloned.1.call-update
  57.2 0.0 all-reduce.9.cloned.1.call-start
  57.3 55.4 %all-reduce.7.cloned.1.call-done = f32[256,128]{0,1:T(8,128)} async-done(((f32[256,128]{0,1:T(8,128)}), f32[256,128]{0,1:T(8,128)}) %all-reduce.7.cloned.1.call-update) | async-done | bytes 131088 | tf_op jit(solution)/shard_map/psum | solution.py:40
  112.7 1.8 convolution_bitcast_fusion.2
  114.5 0.0 all-reduce.9.cloned.1.call-update
  114.5 0.0 all-reduce.11.cloned.1.call-start
  114.5 41.9 %all-reduce.9.cloned.1.call-done = f32[128,128]{0,1:T(8,128)} async-done(((f32[128,128]{0,1:T(8,128)}), f32[128,128]{0,1:T(8,128)}) %all-reduce.9.cloned.1.call-update) | async-done | bytes 65552 | tf_op jit(solution)/shard_map/psum | solution.py:42
  156.5 0.0 copy-done.1
  156.5 0.0 copy-done.3
  156.5 1.5 convolution_bitcast_fusion
  158.0 0.8 copy.8
  158.8 0.0 all-reduce.11.cloned.1.call-update
  158.8 55.6 %all-reduce.11.cloned.1.call-done = f32[4,1,128,128]{3,2,1,0:T(8,128)} async-done(((f32[4,1,128,128]{3,2,1,0:T(8,128)}), f32[4,1,128,128]{3,2,1,0:T(8,128)}) %all-reduce.11.cloned.1.call-update) | async-done | bytes 262160 | tf_op jit(solution)/shard_map/psum | solution.py:46
  214.4 1.0 multiply_reduce_fusion
  215.4 9.8 %psum.39 = f32[128]{0:T(128)S(1)} all-reduce(f32[128]{0:T(128)S(1)} %multiply_reduce_fusion), channel_id=1, replica_groups=mesh['prow'=4,'pcol'=8] {'prow'}, use_global_device_ids=true, to_apply=%region_5.0 | all-reduce | flops 128 | bytes 1024 | tf_op jit(solution)/shard_map/psum | solution.py:47
  225.3 1.4 dynamic-slice_divide_fusion
  (6 shorter events, 0.1 us)
Async XLA Ops:
  6.5 2.5 %copy-start = (f32[4,1,128,256]{3,2,1,0:T(8,128)S(1)}, f32[4,1,128,256]{3,2,1,0:T(8,128)}, u32[]{:S(2)}) copy-start(f32[4,1,128,256]{3,2,1,0:T(8,128)} %param.8) | copy-start | bytes 1572868
  6.5 1.8 copy-start.5
  6.5 48.9 %all-reduce.5.cloned.1.call-start = ((), (), s32[]{:S(2)}) async-start(), calls=%async_computation | async-start | bytes 131072 | tf_op jit(solution)/shard_map/psum | solution.py:42
  8.4 0.7 copy-start.4
  9.1 1.7 copy-start.2
  10.7 102.0 %all-reduce.7.cloned.1.call-start = ((), (), s32[]{:S(2)}) async-start(), calls=%async_computation.1 | async-start | bytes 262144 | tf_op jit(solution)/shard_map/psum | solution.py:40
  10.8 145.7 %copy-start.1 = (f32[4,1,128,2,1,128]{5,4,3,2,1,0:T(1,128)S(1)}, f32[4,1,128,2,1,128]{5,4,3,2,1,0:T(1,128)}, u32[]{:S(2)}) copy-start(f32[4,1,128,2,1,128]{5,4,3,2,1,0:T(1,128)} %param.9) | copy-start | bytes 1572868
  57.2 99.3 %all-reduce.9.cloned.1.call-start = ((), (), s32[]{:S(2)}) async-start(), calls=%async_computation.2 | async-start | bytes 131072 | tf_op jit(solution)/shard_map/psum | solution.py:42
  114.5 42.0 %copy-start.3 = (f32[128,128]{0,1:T(8,128)S(1)}, f32[128,128]{0,1:T(8,128)}, u32[]{:S(2)}) copy-start(f32[128,128]{0,1:T(8,128)} %all-reduce.5.cloned.1.call-done) | copy-start | bytes 196612
  114.5 99.9 %all-reduce.11.cloned.1.call-start = ((), (), s32[]{:S(2)}) async-start(), calls=%async_computation.3 | async-start | bytes 524288 | tf_op jit(solution)/shard_map/psum | solution.py:46
Sparse Core Ops, SparseCore 0:
  10.8 44.5 all-reduce.4
  57.7 54.9 all-reduce.6
  115.5 40.8 all-reduce.8
  158.9 55.4 all-reduce.10
where the time goes:
time: 234 us; the launch traced here: 233 us
  waiting for transfers between devices  198 us (85%)
  between operations  13.2 us (6%)
  blocking collectives  9.84 us (4%)
  matrix products  6.66 us (3%)
  local copies, waits for them, and re-layouts  3.37 us (1%)
  other arithmetic  2.44 us (1%)
    psum x2, waiting for transfers between devices, shards(): pieces[panel_index] = lax.psum(applied, 'prow')  86.5 us
    psum x1, waiting for transfers between devices, shards(): summed = lax.psum(stacked, 'pcol')  55.6 us
    psum x1, waiting for transfers between devices, shards(): residual = residual - lax.psum(partial_value, 'pcol')  55.4 us
    psum x1, blocking collectives, shards(): squares = lax.psum(jnp.sum(summed * summed, axis=(0, 1, 2)), 'prow')  9.84 us
  transfers between devices with their start and end apart: 4, of which 4 were waited for; matrix products, arithmetic and copies ran while one was open for 0% of the time, Pallas kernels for 0%

commit v1 on v0

v1 whole, which is shorter than its diff:
```python
import functools

import jax
import jax.numpy as jnp
from jax import lax
from jax.experimental import pallas as pl
from jax.experimental.pallas import tpu as pltpu
from jax.sharding import PartitionSpec as P

EPSILON = 1e-06
F32 = jnp.float32
BF16 = jnp.bfloat16


def split(x):
    high = x.astype(BF16)
    return high, (x - high.astype(F32)).astype(BF16)


def mm(a, b):
    return jnp.dot(a, b, preferred_element_type=F32)


def dot3(a, b):
    a_high, a_low = split(a)
    b_high, b_low = split(b)
    return mm(a_high, b_high) + (mm(a_high, b_low) + mm(a_low, b_high))


def peers_of(axis, size):
    me = lax.axis_index(axis)
    return me, [lax.rem(me + d, size) for d in range(1, size)]


def send_all(axis, size, source, target, send_sem, recv_sem):
    me, peers = peers_of(axis, size)
    copies = []
    for d, peer in enumerate(peers):
        copy = pltpu.make_async_remote_copy(
            src_ref=source(peer),
            dst_ref=target(d),
            send_sem=send_sem.at[d],
            recv_sem=recv_sem.at[d],
            device_id={axis: peer},
            device_id_type=pl.DeviceIdType.MESH,
        )
        copy.start()
        copies.append(copy)
    return copies


def reduce_scatter(axis, size, parts, landed, send_sem, recv_sem):
    me = lax.axis_index(axis)
    copies = send_all(axis, size, lambda peer: parts.at[peer], lambda d: landed.at[d], send_sem, recv_sem)
    total = parts[me]
    for d, copy in enumerate(copies):
        copy.wait_recv()
        total = total + landed[d]
    return total, copies


def all_gather(axis, size, whole, send_sem, recv_sem):
    me = lax.axis_index(axis)
    return send_all(axis, size, lambda peer: whole.at[me], lambda d: whole.at[me], send_sem, recv_sem)


def kernel(
    sizes,
    schur_ref, inverse_ref, coupling_ref, z_ref, targets_ref, flags_ref,
    out_ref,
    s_mem, m_mem, c_mem, z_mem, load_sem,
    a_parts, a_landed, a_whole, b_parts, b_landed, b_whole,
    c_parts, c_landed, c_whole, d_parts, d_landed, e_own, e_row, e_col,
    a_ss, a_rs, a_sg, a_rg, b_ss, b_rs, b_sg, b_rg,
    c_ss, c_rs, c_sg, c_rg, d_ss, d_rs, e_ss, e_rs, e_sg, e_rg,
):
    n_row, n_col, block, strip, window, count, z_blocks = sizes
    share = block // n_col
    barrier = pltpu.get_barrier_semaphore()
    row, row_peers = peers_of("prow", n_row)
    col, col_peers = peers_of("pcol", n_col)
    for peer in row_peers:
        pl.semaphore_signal(barrier, inc=1, device_id={"prow": peer}, device_id_type=pl.DeviceIdType.MESH)
    for peer in col_peers:
        pl.semaphore_signal(barrier, inc=1, device_id={"pcol": peer}, device_id_type=pl.DeviceIdType.MESH)
    loads = [
        pltpu.make_async_copy(coupling_ref, c_mem, load_sem.at[0]),
        pltpu.make_async_copy(inverse_ref, m_mem, load_sem.at[1]),
        pltpu.make_async_copy(schur_ref.at[pl.ds(0, 2 * strip)], s_mem, load_sem.at[2]),
        pltpu.make_async_copy(z_ref, z_mem, load_sem.at[3]),
    ]
    for load in loads:
        load.start()
    columns = lax.broadcasted_iota(jnp.int32, (window, count), 0)
    targets = targets_ref[...]
    selection = (columns == targets).astype(F32) + flags_ref[...].astype(F32) * (columns == targets + 1).astype(F32)
    selection = selection.astype(BF16)

    def right_side(panel):
        c_high, c_low = split(c_mem[pl.ds(panel * strip, strip), :])
        return -(mm(c_high, selection) + mm(c_low, selection))

    def apply_inverse(panel, residual):
        total = None
        for part in range(strip // block):
            piece = m_mem[pl.ds(panel * block * 2 + part, block, stride=2), :]
            term = dot3(piece, residual[part * block : (part + 1) * block])
            total = term if total is None else total + term
        return total

    loads[0].wait()
    side = right_side(1)
    loads[1].wait()
    applied = apply_inverse(1, side)
    a_parts[...] = applied.reshape(a_parts.shape)
    pl.semaphore_wait(barrier, n_row + n_col - 2)

    total, a_sent = reduce_scatter("prow", n_row, a_parts, a_landed, a_ss, a_rs)
    a_whole[row] = total
    a_gather = all_gather("prow", n_row, a_whole, a_sg, a_rg)
    side = right_side(0)
    loads[2].wait()
    loads[3].wait()
    for copy in a_gather:
        copy.wait_recv()
    later = a_whole[...].reshape(block, count)

    partial = dot3(s_mem[pl.ds(1, strip, stride=2), :], later)
    b_parts[...] = partial.reshape(b_parts.shape)
    total, b_sent = reduce_scatter("pcol", n_col, b_parts, b_landed, b_ss, b_rs)
    b_whole[col] = total
    b_gather = all_gather("pcol", n_col, b_whole, b_sg, b_rg)
    z_later = dot3(z_mem[pl.ds(1, z_blocks * block, stride=2), :], later)
    for copy in b_gather:
        copy.wait_recv()
    residual = side - b_whole[...].reshape(strip, count)

    applied = apply_inverse(0, residual)
    c_parts[...] = applied.reshape(c_parts.shape)
    total, c_sent = reduce_scatter("prow", n_row, c_parts, c_landed, c_ss, c_rs)
    c_whole[row] = total
    c_gather = all_gather("prow", n_row, c_whole, c_sg, c_rg)
    for copy in c_gather:
        copy.wait_recv()
    first = c_whole[...].reshape(block, count)

    transformed = z_later + dot3(z_mem[pl.ds(0, z_blocks * block, stride=2), :], first)
    for peer in range(n_col):
        for z_block in range(z_blocks):
            start = z_block * block + peer * share
            d_parts[peer, z_block] = transformed[start : start + share]
    owned, d_sent = reduce_scatter("pcol", n_col, d_parts, d_landed, d_ss, d_rs)
    squares = jnp.sum(jnp.sum(owned * owned, axis=0), axis=0, keepdims=True)
    e_own[0] = squares
    e_sent = send_all("prow", n_row, lambda peer: e_own.at[0], lambda d: e_row.at[d], e_ss, e_rs)
    for d, copy in enumerate(e_sent):
        copy.wait_recv()
        squares = squares + e_row[d]
    e_own[1] = squares
    e_gather = send_all("pcol", n_col, lambda peer: e_own.at[1], lambda d: e_col.at[d], e_sg, e_rg)
    for d, copy in enumerate(e_gather):
        copy.wait_recv()
        squares = squares + e_col[d]
    rows = z_blocks * block * n_row
    divisor = jnp.sqrt(squares / rows + EPSILON)
    out_ref[...] = owned / divisor[None]
    for copy in a_sent + a_gather + b_sent + b_gather + c_sent + c_gather + d_sent + e_sent + e_gather:
        copy.wait_send()


def shards(n_row, n_col, schur, panel_inverse, coupling, zslab, targets, pair_flags):
    block = schur.shape[2]
    strip = panel_inverse.shape[3] * block
    window = coupling.shape[3]
    count = targets.shape[0]
    z_blocks = zslab.shape[0]
    share = block // n_col
    sizes = (n_row, n_col, block, strip, window, count, z_blocks)
    flat = lambda x: x.reshape(-1, block)
    dma = lambda n: pltpu.SemaphoreType.DMA((n - 1,))
    row_sems = [dma(n_row)] * 4
    col_sems = [dma(n_col)] * 4

    def buffers(size, height):
        piece = (height // size, count)
        return [
            pltpu.VMEM((size,) + piece, F32),
            pltpu.VMEM((size - 1,) + piece, F32),
            pltpu.VMEM((size,) + piece, F32),
        ]

    anywhere = pl.BlockSpec(memory_space=pl.ANY)
    local = pl.BlockSpec(memory_space=pltpu.VMEM)
    out = pl.pallas_call(
        functools.partial(kernel, sizes),
        out_shape=jax.ShapeDtypeStruct((z_blocks, share, count), F32),
        in_specs=[anywhere] * 4 + [local] * 2,
        out_specs=local,
        scratch_shapes=[
            pltpu.VMEM((2 * strip, block), F32),
            pltpu.VMEM((panel_inverse.size // block, block), F32),
            pltpu.VMEM((coupling.size // window, window), F32),
            pltpu.VMEM((zslab.size // block, block), F32),
            pltpu.SemaphoreType.DMA((4,)),
        ]
        + buffers(n_row, block)
        + buffers(n_col, strip)
        + buffers(n_row, block)
        + [
            pltpu.VMEM((n_col, z_blocks, share, count), F32),
            pltpu.VMEM((n_col - 1, z_blocks, share, count), F32),
            pltpu.VMEM((2, 1, count), F32),
            pltpu.VMEM((n_row - 1, 1, count), F32),
            pltpu.VMEM((n_col - 1, 1, count), F32),
        ]
        + row_sems
        + col_sems
        + row_sems
        + [dma(n_col)] * 2
        + [dma(n_row)] * 2
        + [dma(n_col)] * 2,
        compiler_params=pltpu.CompilerParams(collective_id=0, has_side_effects=True, vmem_limit_bytes=60 * 1024 * 1024),
    )(
        flat(schur),
        flat(panel_inverse),
        coupling.reshape(-1, window),
        flat(zslab),
        targets.reshape(1, -1),
        pair_flags.reshape(1, -1),
    )
    return out.reshape(z_blocks, 1, share, count)


def solution(mesh):
    in_specs = (
        P(None, "prow", None, None, "pcol", None),
        P(None, "pcol", None, None, "prow", None),
        P(None, "prow", None, None),
        P(None, "prow", None, None, "pcol", None),
        P(),
        P(),
    )
    out_specs = P(None, "prow", "pcol", None)
    body = functools.partial(shards, mesh.shape["prow"], mesh.shape["pcol"])
    return jax.shard_map(body, mesh=mesh, in_specs=in_specs, out_specs=out_specs, check_vma=False)
```

time: 234 us -> 44.5 us (0.19)
  waiting for transfers between devices: 198 us -> 0 us
  Pallas kernels: 0 us -> 42.9 us
  between operations: 13.2 us -> 0.01 us
  blocking collectives: 9.84 us -> 0 us
  matrix products: 6.66 us -> 0 us
  other arithmetic: 2.44 us -> 0 us
    psum x4 -> x0, waiting for transfers between devices: 197 us -> none  [the longest x2 86.5 us: shards(): pieces[panel_index] = lax.psum(applied, 'prow')]
    pallas_call x0 -> x1, Pallas kernels: none -> 42.9 us  [shards(): pl.pallas_call(functools.partial(kernel, sizes), out_shape=jax.ShapeDtype...]
    psum x1 -> x0, blocking collectives: 9.84 us -> none  [shards(): squares = lax.psum(jnp.sum(summed * summed, axis=(0, 1, 2)), 'prow')]
    dot_general x5 -> x0, matrix products: 6.66 us -> none  [the longest x2 2.7 us: shards(): jnp.dot(inverse[panel_index], residual, precision=lax.Precision.HIGHEST)]
  transfers between devices with their start and end apart: 4 -> 0, of which waited for: 4 -> 0; matrix products, arithmetic and copies ran while one was open for 0% -> 0% of each run, Pallas kernels for 0% -> 0%
where the time goes in v1:
time: 44.5 us; the launch traced here: 44.3 us
  Pallas kernels  42.9 us (96%)
  local copies, waits for them, and re-layouts  1.38 us (3%)
    pallas_call x1, Pallas kernels, shards(): pl.pallas_call(functools.partial(kernel, sizes), out_shape=jax.ShapeDtype...  42.9 us
    unnamed x1, local copies, waits for them, and re-layouts  1.38 us

profile of v1, /device:TPU:0, one launch (start us, length us, event | category | flops | bytes accessed | tf_op | source)
XLA Modules:
  0.0 44.3 jit_solution(3482413463936191905)
XLA Ops:
  0.0 42.9 %shard_map.64 = f32[4,16,128]{2,1,0:T(8,128)} custom-call(f32[1024,128]{1,0:T(8,128)} %bitcast.9, f32[512,128]{1,0:T(8,128)} %bitcast.12, f32[512,256]{1,0:T(8,128)} %bitcast.10, f32[1024,128]{1,0:T(8,128)} %bitcast.11, s32[1,128]{1,0:T(1,128)} %bitcast.14, s32[1,128]{1,0:T(1,128)} %bitcast.15), custom_call_target="tpu_custom_call" | custom-call | tf_op jit(solution)/shard_map/pallas_call | solution.py:194
  42.9 1.4 %copy.9 = f32[4,1,16,128]{3,2,1,0:T(8,128)} copy(f32[4,1,16,128]{3,2,1,0:T(8,128)} %bitcast.13) | data formatting | bytes 65536

commit v2 on v1

--- a/solution.py
+++ b/solution.py
@@ -10,6 +10,7 @@
 EPSILON = 1e-06
 F32 = jnp.float32
 BF16 = jnp.bfloat16
+DIRECT_LIMIT = 64
 
 
 def split(x):
@@ -69,20 +70,24 @@
     schur_ref, inverse_ref, coupling_ref, z_ref, targets_ref, flags_ref,
     out_ref,
     s_mem, m_mem, c_mem, z_mem, load_sem,
-    a_parts, a_landed, a_whole, b_parts, b_landed, b_whole,
-    c_parts, c_landed, c_whole, d_parts, d_landed, e_own, e_row, e_col,
-    a_ss, a_rs, a_sg, a_rg, b_ss, b_rs, b_sg, b_rg,
-    c_ss, c_rs, c_sg, c_rg, d_ss, d_rs, e_ss, e_rs, e_sg, e_rg,
+    a_own, a_landed, b_parts, b_landed, b_whole, c_own, c_landed,
+    d_parts, d_pair, d_sum, d_landed, e_own, e_row, e_col,
+    a_ss, a_rs, b_ss, b_rs, b_sg, b_rg, c_ss, c_rs,
+    p_ss, p_rs, d_ss, d_rs, e_ss, e_rs, e_sg, e_rg,
 ):
     n_row, n_col, block, strip, window, count, z_blocks = sizes
     share = block // n_col
     barrier = pltpu.get_barrier_semaphore()
     row, row_peers = peers_of("prow", n_row)
     col, col_peers = peers_of("pcol", n_col)
-    for peer in row_peers:
-        pl.semaphore_signal(barrier, inc=1, device_id={"prow": peer}, device_id_type=pl.DeviceIdType.MESH)
-    for peer in col_peers:
-        pl.semaphore_signal(barrier, inc=1, device_id={"pcol": peer}, device_id_type=pl.DeviceIdType.MESH)
+    n_chip = n_col // 2
+    direct = n_row * n_col <= DIRECT_LIMIT
+    all_peers = [
+        (lax.rem(row + i, n_row), lax.rem(col + j, n_col)) for i in range(n_row) for j in range(n_col) if i + j > 0
+    ]
+    greeted = all_peers if direct else [(peer, col) for peer in row_peers] + [(row, peer) for peer in col_peers]
+    for peer in greeted:
+        pl.semaphore_signal(barrier, inc=1, device_id=peer, device_id_type=pl.DeviceIdType.MESH)
     loads = [
         pltpu.make_async_copy(coupling_ref, c_mem, load_sem.at[0]),
         pltpu.make_async_copy(inverse_ref, m_mem, load_sem.at[1]),
@@ -112,18 +117,17 @@
     side = right_side(1)
     loads[1].wait()
     applied = apply_inverse(1, side)
-    a_parts[...] = applied.reshape(a_parts.shape)
-    pl.semaphore_wait(barrier, n_row + n_col - 2)
-
-    total, a_sent = reduce_scatter("prow", n_row, a_parts, a_landed, a_ss, a_rs)
-    a_whole[row] = total
-    a_gather = all_gather("prow", n_row, a_whole, a_sg, a_rg)
+    a_own[...] = applied
+    pl.semaphore_wait(barrier, len(greeted))
+
+    a_sent = send_all("prow", n_row, lambda peer: a_own, lambda d: a_landed.at[d], a_ss, a_rs)
     side = right_side(0)
     loads[2].wait()
     loads[3].wait()
-    for copy in a_gather:
-        copy.wait_recv()
-    later = a_whole[...].reshape(block, count)
+    later = applied
+    for d, copy in enumerate(a_sent):
+        copy.wait_recv()
+        later = later + a_landed[d]
 
     partial = dot3(s_mem[pl.ds(1, strip, stride=2), :], later)
     b_parts[...] = partial.reshape(b_parts.shape)
@@ -136,35 +140,91 @@
     residual = side - b_whole[...].reshape(strip, count)
 
     applied = apply_inverse(0, residual)
-    c_parts[...] = applied.reshape(c_parts.shape)
-    total, c_sent = reduce_scatter("prow", n_row, c_parts, c_landed, c_ss, c_rs)
-    c_whole[row] = total
-    c_gather = all_gather("prow", n_row, c_whole, c_sg, c_rg)
-    for copy in c_gather:
-        copy.wait_recv()
-    first = c_whole[...].reshape(block, count)
+    c_own[...] = applied
+    c_sent = send_all("prow", n_row, lambda peer: c_own, lambda d: c_landed.at[d], c_ss, c_rs)
+    first = applied
+    for d, copy in enumerate(c_sent):
+        copy.wait_recv()
+        first = first + c_landed[d]
 
     transformed = z_later + dot3(z_mem[pl.ds(0, z_blocks * block, stride=2), :], first)
     for peer in range(n_col):
         for z_block in range(z_blocks):
             start = z_block * block + peer * share
-            d_parts[peer, z_block] = transformed[start : start + share]
-    owned, d_sent = reduce_scatter("pcol", n_col, d_parts, d_landed, d_ss, d_rs)
+            d_parts[peer % 2, peer // 2, z_block] = transformed[start : start + share]
+    core, chip = lax.rem(col, 2), col // 2
+    places = [lax.rem(chip + d, n_chip) for d in range(1, n_chip)] + [chip]
+    pair_sent = []
+    for d, place in enumerate(places):
+        copy = pltpu.make_async_remote_copy(
+            src_ref=d_parts.at[1 - core, place],
+            dst_ref=d_pair.at[place],
+            send_sem=p_ss.at[d],
+            recv_sem=p_rs.at[place],
+            device_id={"pcol": col + 1 - 2 * core},
+            device_id_type=pl.DeviceIdType.MESH,
+        )
+        copy.start()
+        pair_sent.append(copy)
+    d_sent = []
+    for d, place in enumerate(places):
+        pltpu.make_async_remote_copy(
+            src_ref=d_parts.at[1 - core, place],
+            dst_ref=d_pair.at[place],
+            send_sem=p_ss.at[d],
+            recv_sem=p_rs.at[place],
+            device_id={"pcol": col + 1 - 2 * core},
+            device_id_type=pl.DeviceIdType.MESH,
+        ).wait_recv()
+        owned = d_parts[core, place] + d_pair[place]
+        if d < n_chip - 1:
+            d_sum[d] = owned
+            copy = pltpu.make_async_remote_copy(
+                src_ref=d_sum.at[d],
+                dst_ref=d_landed.at[d],
+                send_sem=d_ss.at[d],
+                recv_sem=d_rs.at[d],
+                device_id={"pcol": 2 * place + core},
+                device_id_type=pl.DeviceIdType.MESH,
+            )
+            copy.start()
+            d_sent.append(copy)
+    for d, copy in enumerate(d_sent):
+        copy.wait_recv()
+        owned = owned + d_landed[d]
     squares = jnp.sum(jnp.sum(owned * owned, axis=0), axis=0, keepdims=True)
     e_own[0] = squares
-    e_sent = send_all("prow", n_row, lambda peer: e_own.at[0], lambda d: e_row.at[d], e_ss, e_rs)
-    for d, copy in enumerate(e_sent):
-        copy.wait_recv()
-        squares = squares + e_row[d]
-    e_own[1] = squares
-    e_gather = send_all("pcol", n_col, lambda peer: e_own.at[1], lambda d: e_col.at[d], e_sg, e_rg)
-    for d, copy in enumerate(e_gather):
-        copy.wait_recv()
-        squares = squares + e_col[d]
+    if direct:
+        e_sent = []
+        for d, peer in enumerate(all_peers):
+            copy = pltpu.make_async_remote_copy(
+                src_ref=e_own.at[0],
+                dst_ref=e_col.at[d],
+                send_sem=e_sg.at[d],
+                recv_sem=e_rg.at[d],
+                device_id=peer,
+                device_id_type=pl.DeviceIdType.MESH,
+            )
+            copy.start()
+            e_sent.append(copy)
+        for copy in e_sent:
+            copy.wait_recv()
+        squares = squares + jnp.sum(e_col[...], axis=0)
+        e_gather = []
+    else:
+        e_sent = send_all("prow", n_row, lambda peer: e_own.at[0], lambda d: e_row.at[d], e_ss, e_rs)
+        for d, copy in enumerate(e_sent):
+            copy.wait_recv()
+            squares = squares + e_row[d]
+        e_own[1] = squares
+        e_gather = send_all("pcol", n_col, lambda peer: e_own.at[1], lambda d: e_col.at[d], e_sg, e_rg)
+        for d, copy in enumerate(e_gather):
+            copy.wait_recv()
+            squares = squares + e_col[d]
     rows = z_blocks * block * n_row
     divisor = jnp.sqrt(squares / rows + EPSILON)
     out_ref[...] = owned / divisor[None]
-    for copy in a_sent + a_gather + b_sent + b_gather + c_sent + c_gather + d_sent + e_sent + e_gather:
+    for copy in a_sent + b_sent + b_gather + c_sent + pair_sent + d_sent + e_sent + e_gather:
         copy.wait_send()
 
 
@@ -178,15 +238,17 @@
     sizes = (n_row, n_col, block, strip, window, count, z_blocks)
     flat = lambda x: x.reshape(-1, block)
     dma = lambda n: pltpu.SemaphoreType.DMA((n - 1,))
-    row_sems = [dma(n_row)] * 4
-    col_sems = [dma(n_col)] * 4
+    n_chip = n_col // 2
+    last = n_row * n_col if n_row * n_col <= DIRECT_LIMIT else n_col
+    piece = (z_blocks, share, count)
+    direct_buffers = [pltpu.VMEM((block, count), F32), pltpu.VMEM((n_row - 1, block, count), F32)]
 
     def buffers(size, height):
-        piece = (height // size, count)
+        rows = (height // size, count)
         return [
-            pltpu.VMEM((size,) + piece, F32),
-            pltpu.VMEM((size - 1,) + piece, F32),
-            pltpu.VMEM((size,) + piece, F32),
+            pltpu.VMEM((size,) + rows, F32),
+            pltpu.VMEM((size - 1,) + rows, F32),
+            pltpu.VMEM((size,) + rows, F32),
         ]
 
     anywhere = pl.BlockSpec(memory_space=pl.ANY)
@@ -203,22 +265,25 @@
             pltpu.VMEM((zslab.size // block, block), F32),
             pltpu.SemaphoreType.DMA((4,)),
         ]
-        + buffers(n_row, block)
+        + direct_buffers
         + buffers(n_col, strip)
-        + buffers(n_row, block)
+        + direct_buffers
         + [
-            pltpu.VMEM((n_col, z_blocks, share, count), F32),
-            pltpu.VMEM((n_col - 1, z_blocks, share, count), F32),
+            pltpu.VMEM((2, n_chip) + piece, F32),
+            pltpu.VMEM((n_chip,) + piece, F32),
+            pltpu.VMEM((n_chip - 1,) + piece, F32),
+            pltpu.VMEM((n_chip - 1,) + piece, F32),
             pltpu.VMEM((2, 1, count), F32),
             pltpu.VMEM((n_row - 1, 1, count), F32),
-            pltpu.VMEM((n_col - 1, 1, count), F32),
+            pltpu.VMEM((last - 1, 1, count), F32),
         ]
-        + row_sems
-        + col_sems
-        + row_sems
-        + [dma(n_col)] * 2
         + [dma(n_row)] * 2
-        + [dma(n_col)] * 2,
+        + [dma(n_col)] * 4
+        + [dma(n_row)] * 2
+        + [dma(n_chip + 1)] * 2
+        + [dma(n_chip)] * 2
+        + [dma(n_row)] * 2
+        + [dma(last)] * 2,
         compiler_params=pltpu.CompilerParams(collective_id=0, has_side_effects=True, vmem_limit_bytes=60 * 1024 * 1024),
     )(
         flat(schur),

time: 44.5 us -> 40.2 us (0.903)
  Pallas kernels: 42.9 us -> 38.6 us
    pallas_call x1, Pallas kernels: 42.9 us -> 38.6 us  [shards(): pl.pallas_call(functools.partial(kernel, sizes), out_shape=jax.ShapeDtype...]
where the time goes in v2:
time: 40.2 us; the launch traced here: 40 us
  Pallas kernels  38.6 us (96%)
  local copies, waits for them, and re-layouts  1.38 us (3%)
    pallas_call x1, Pallas kernels, shards(): pl.pallas_call(functools.partial(kernel, sizes), out_shape=jax.ShapeDtype...  38.6 us
    unnamed x1, local copies, waits for them, and re-layouts  1.38 us

profile of v2, /device:TPU:0, one launch (start us, length us, event | category | flops | bytes accessed | tf_op | source)
XLA Modules:
  0.0 40.0 jit_solution(8509916484406553793)
XLA Ops:
  0.0 38.6 %shard_map.64 = f32[4,16,128]{2,1,0:T(8,128)} custom-call(f32[1024,128]{1,0:T(8,128)} %bitcast.9, f32[512,128]{1,0:T(8,128)} %bitcast.12, f32[512,256]{1,0:T(8,128)} %bitcast.10, f32[1024,128]{1,0:T(8,128)} %bitcast.11, s32[1,128]{1,0:T(1,128)} %bitcast.14, s32[1,128]{1,0:T(1,128)} %bitcast.15), custom_call_target="tpu_custom_call" | custom-call | tf_op jit(solution)/shard_map/pallas_call | solution.py:256
  38.6 1.4 %copy.9 = f32[4,1,16,128]{3,2,1,0:T(8,128)} copy(f32[4,1,16,128]{3,2,1,0:T(8,128)} %bitcast.13) | data formatting | bytes 65536

commit v3 on v2

--- a/solution.py
+++ b/solution.py
@@ -11,6 +11,7 @@
 F32 = jnp.float32
 BF16 = jnp.bfloat16
 DIRECT_LIMIT = 64
+VMEM_LIMIT = 67043328
 
 
 def split(x):
@@ -28,9 +29,24 @@
     return mm(a_high, b_high) + (mm(a_high, b_low) + mm(a_low, b_high))
 
 
+def exclusive_or(number, mask):
+    result, bit = 0, 1
+    while bit <= mask:
+        digit = lax.rem(number // bit, 2)
+        result = result + bit * (1 - digit if mask & bit else digit)
+        bit *= 2
+    return result + number // bit * bit
+
+
+def partners(number, size):
+    if size & (size - 1):
+        raise ValueError("axis size")
+    return [exclusive_or(number, mask) for mask in reversed(range(1, size))]
+
+
 def peers_of(axis, size):
     me = lax.axis_index(axis)
-    return me, [lax.rem(me + d, size) for d in range(1, size)]
+    return me, partners(me, size)
 
 
 def send_all(axis, size, source, target, send_sem, recv_sem):
@@ -69,7 +85,7 @@
     sizes,
     schur_ref, inverse_ref, coupling_ref, z_ref, targets_ref, flags_ref,
     out_ref,
-    s_mem, m_mem, c_mem, z_mem, load_sem,
+    s_mem, m_mem, c_mem, z_mem, t_mem, load_sem,
     a_own, a_landed, b_parts, b_landed, b_whole, c_own, c_landed,
     d_parts, d_pair, d_sum, d_landed, e_own, e_row, e_col,
     a_ss, a_rs, b_ss, b_rs, b_sg, b_rg, c_ss, c_rs,
@@ -82,13 +98,13 @@
     col, col_peers = peers_of("pcol", n_col)
     n_chip = n_col // 2
     direct = n_row * n_col <= DIRECT_LIMIT
-    all_peers = [
-        (lax.rem(row + i, n_row), lax.rem(col + j, n_col)) for i in range(n_row) for j in range(n_col) if i + j > 0
-    ]
-    greeted = all_peers if direct else [(peer, col) for peer in row_peers] + [(row, peer) for peer in col_peers]
+    all_peers = [(i, j) for j in col_peers + [col] for i in row_peers + [row]][:-1]
+    greeted = [(peer, col) for peer in row_peers] + [(row, peer) for peer in col_peers]
     for peer in greeted:
         pl.semaphore_signal(barrier, inc=1, device_id=peer, device_id_type=pl.DeviceIdType.MESH)
     loads = [
+        pltpu.make_async_copy(targets_ref, t_mem.at[0], load_sem.at[4]),
+        pltpu.make_async_copy(flags_ref, t_mem.at[1], load_sem.at[5]),
         pltpu.make_async_copy(coupling_ref, c_mem, load_sem.at[0]),
         pltpu.make_async_copy(inverse_ref, m_mem, load_sem.at[1]),
         pltpu.make_async_copy(schur_ref.at[pl.ds(0, 2 * strip)], s_mem, load_sem.at[2]),
@@ -96,9 +112,12 @@
     ]
     for load in loads:
         load.start()
+    loads[0].wait()
+    loads[1].wait()
+    loads = loads[2:]
     columns = lax.broadcasted_iota(jnp.int32, (window, count), 0)
-    targets = targets_ref[...]
-    selection = (columns == targets).astype(F32) + flags_ref[...].astype(F32) * (columns == targets + 1).astype(F32)
+    targets = t_mem[0]
+    selection = (columns == targets).astype(F32) + t_mem[1].astype(F32) * (columns == targets + 1).astype(F32)
     selection = selection.astype(BF16)
 
     def right_side(panel):
@@ -153,7 +172,7 @@
             start = z_block * block + peer * share
             d_parts[peer % 2, peer // 2, z_block] = transformed[start : start + share]
     core, chip = lax.rem(col, 2), col // 2
-    places = [lax.rem(chip + d, n_chip) for d in range(1, n_chip)] + [chip]
+    places = partners(chip, n_chip) + [chip]
     pair_sent = []
     for d, place in enumerate(places):
         copy = pltpu.make_async_remote_copy(
@@ -221,9 +240,7 @@
         for d, copy in enumerate(e_gather):
             copy.wait_recv()
             squares = squares + e_col[d]
-    rows = z_blocks * block * n_row
-    divisor = jnp.sqrt(squares / rows + EPSILON)
-    out_ref[...] = owned / divisor[None]
+    out_ref[...] = owned / jnp.sqrt(squares / (z_blocks * block * n_row) + EPSILON)[None]
     for copy in a_sent + b_sent + b_gather + c_sent + pair_sent + d_sent + e_sent + e_gather:
         copy.wait_send()
 
@@ -255,15 +272,16 @@
     local = pl.BlockSpec(memory_space=pltpu.VMEM)
     out = pl.pallas_call(
         functools.partial(kernel, sizes),
-        out_shape=jax.ShapeDtypeStruct((z_blocks, share, count), F32),
-        in_specs=[anywhere] * 4 + [local] * 2,
+        out_shape=jax.ShapeDtypeStruct(piece, F32),
+        in_specs=[anywhere] * 6,
         out_specs=local,
         scratch_shapes=[
             pltpu.VMEM((2 * strip, block), F32),
             pltpu.VMEM((panel_inverse.size // block, block), F32),
             pltpu.VMEM((coupling.size // window, window), F32),
             pltpu.VMEM((zslab.size // block, block), F32),
-            pltpu.SemaphoreType.DMA((4,)),
+            pltpu.VMEM((2, 1, count), jnp.int32),
+            pltpu.SemaphoreType.DMA((6,)),
         ]
         + direct_buffers
         + buffers(n_col, strip)
@@ -284,7 +302,7 @@
         + [dma(n_chip)] * 2
         + [dma(n_row)] * 2
         + [dma(last)] * 2,
-        compiler_params=pltpu.CompilerParams(collective_id=0, has_side_effects=True, vmem_limit_bytes=60 * 1024 * 1024),
+        compiler_params=pltpu.CompilerParams(collective_id=0, has_side_effects=True, vmem_limit_bytes=VMEM_LIMIT),
     )(
         flat(schur),
         flat(panel_inverse),

time: 40.2 us -> 38 us (0.945)
  Pallas kernels: 38.6 us -> 36.4 us
    pallas_call x1, Pallas kernels: 38.6 us -> 36.4 us  [shards(): pl.pallas_call(functools.partial(kernel, sizes), out_shape=jax.ShapeDtype...]
where the time goes in v3:
time: 38 us; the launch traced here: 37.8 us
  Pallas kernels  36.4 us (96%)
  local copies, waits for them, and re-layouts  1.38 us (4%)
    pallas_call x1, Pallas kernels, shards(): pl.pallas_call(functools.partial(kernel, sizes), out_shape=jax.ShapeDtype...  36.4 us
    unnamed x1, local copies, waits for them, and re-layouts  1.38 us

profile of v3, /device:TPU:0, one launch (start us, length us, event | category | flops | bytes accessed | tf_op | source)
XLA Modules:
  0.0 37.8 jit_solution(4163756441159835628)
XLA Ops:
  0.0 36.4 %shard_map.64 = f32[4,16,128]{2,1,0:T(8,128)} custom-call(f32[1024,128]{1,0:T(8,128)} %bitcast.9, f32[512,128]{1,0:T(8,128)} %bitcast.12, f32[512,256]{1,0:T(8,128)} %bitcast.10, f32[1024,128]{1,0:T(8,128)} %bitcast.11, s32[1,128]{1,0:T(1,128)} %bitcast.14, s32[1,128]{1,0:T(1,128)} %bitcast.15), custom_call_target="tpu_custom_call" | custom-call | tf_op jit(solution)/shard_map/pallas_call | solution.py:273
  36.4 1.4 %copy.9 = f32[4,1,16,128]{3,2,1,0:T(8,128)} copy(f32[4,1,16,128]{3,2,1,0:T(8,128)} %bitcast.13) | data formatting | bytes 65536

commit v4 on v3

--- a/solution.py
+++ b/solution.py
@@ -85,7 +85,7 @@
     sizes,
     schur_ref, inverse_ref, coupling_ref, z_ref, targets_ref, flags_ref,
     out_ref,
-    s_mem, m_mem, c_mem, z_mem, t_mem, load_sem,
+    s_mem, m_mem, c_mem, z_mem, t_mem, load_sem, relay_sem,
     a_own, a_landed, b_parts, b_landed, b_whole, c_own, c_landed,
     d_parts, d_pair, d_sum, d_landed, e_own, e_row, e_col,
     a_ss, a_rs, b_ss, b_rs, b_sg, b_rg, c_ss, c_rs,
@@ -99,9 +99,34 @@
     n_chip = n_col // 2
     direct = n_row * n_col <= DIRECT_LIMIT
     all_peers = [(i, j) for j in col_peers + [col] for i in row_peers + [row]][:-1]
-    greeted = [(peer, col) for peer in row_peers] + [(row, peer) for peer in col_peers]
-    for peer in greeted:
-        pl.semaphore_signal(barrier, inc=1, device_id=peer, device_id_type=pl.DeviceIdType.MESH)
+    core, chip = lax.rem(col, 2), col // 2
+
+    def greet(semaphore, reach):
+        near = 1
+        pl.semaphore_signal(
+            semaphore, inc=1, device_id={"pcol": col + 1 - 2 * core}, device_id_type=pl.DeviceIdType.MESH
+        )
+        for step in range(-min(reach, n_chip - 1), min(reach, n_chip - 1) + 1):
+            if step:
+                place = chip + step
+                inside = jnp.logical_and(place >= 0, place < n_chip)
+
+                @pl.when(inside)
+                def _():
+                    for other in range(2):
+                        pl.semaphore_signal(
+                            semaphore,
+                            inc=1,
+                            device_id={"pcol": 2 * place + other},
+                            device_id_type=pl.DeviceIdType.MESH,
+                        )
+
+                near = near + jnp.where(inside, 2, 0)
+        return near
+
+    for peer in row_peers:
+        pl.semaphore_signal(barrier, inc=1, device_id={"prow": peer}, device_id_type=pl.DeviceIdType.MESH)
+    near = greet(barrier, 1)
     loads = [
         pltpu.make_async_copy(targets_ref, t_mem.at[0], load_sem.at[4]),
         pltpu.make_async_copy(flags_ref, t_mem.at[1], load_sem.at[5]),
@@ -137,10 +162,12 @@
     loads[1].wait()
     applied = apply_inverse(1, side)
     a_own[...] = applied
-    pl.semaphore_wait(barrier, len(greeted))
+    pl.semaphore_wait(barrier, n_row - 1 + near)
 
     a_sent = send_all("prow", n_row, lambda peer: a_own, lambda d: a_landed.at[d], a_ss, a_rs)
     side = right_side(0)
+    for index in range((n_chip - 1).bit_length()):
+        pl.semaphore_wait(relay_sem.at[index], greet(relay_sem.at[index], 2**index))
     loads[2].wait()
     loads[3].wait()
     later = applied
@@ -282,6 +309,7 @@
             pltpu.VMEM((zslab.size // block, block), F32),
             pltpu.VMEM((2, 1, count), jnp.int32),
             pltpu.SemaphoreType.DMA((6,)),
+            pltpu.SemaphoreType.REGULAR((max((n_chip - 1).bit_length(), 1),)),
         ]
         + direct_buffers
         + buffers(n_col, strip)

time: 38 us -> 37.5 us (0.987)
  Pallas kernels: 36.4 us -> 35.9 us
    pallas_call x1, Pallas kernels: 36.4 us -> 35.9 us  [shards(): pl.pallas_call(functools.partial(kernel, sizes), out_shape=jax.ShapeDtype...]
where the time goes in v4:
time: 37.5 us; the launch traced here: 37.3 us
  Pallas kernels  35.9 us (96%)
  local copies, waits for them, and re-layouts  1.38 us (4%)
    pallas_call x1, Pallas kernels, shards(): pl.pallas_call(functools.partial(kernel, sizes), out_shape=jax.ShapeDtype...  35.9 us
    unnamed x1, local copies, waits for them, and re-layouts  1.38 us

profile of v4, /device:TPU:0, one launch (start us, length us, event | category | flops | bytes accessed | tf_op | source)
XLA Modules:
  0.0 37.3 jit_solution(18378805479058685853)
XLA Ops:
  0.0 35.9 %shard_map.64 = f32[4,16,128]{2,1,0:T(8,128)} custom-call(f32[1024,128]{1,0:T(8,128)} %bitcast.9, f32[512,128]{1,0:T(8,128)} %bitcast.12, f32[512,256]{1,0:T(8,128)} %bitcast.10, f32[1024,128]{1,0:T(8,128)} %bitcast.11, s32[1,128]{1,0:T(1,128)} %bitcast.14, s32[1,128]{1,0:T(1,128)} %bitcast.15), custom_call_target="tpu_custom_call" | custom-call | tf_op jit(solution)/shard_map/pallas_call | solution.py:300
  35.9 1.4 %copy.9 = f32[4,1,16,128]{3,2,1,0:T(8,128)} copy(f32[4,1,16,128]{3,2,1,0:T(8,128)} %bitcast.13) | data formatting | bytes 65536
